TPU v7x, 32 devices: a whole 2x2x4 slice. The times are simulated.
32 devices in a mesh: seq: 4 (over y, x), grp: 8 (over z, core).
Axes of the slice: x: 2, y: 2, z: 4, core: 2. Of those that a mesh axis runs over, the one named last changes fastest.
Arguments:
- tokens: bfloat16 [16384, 768], P(('grp', 'seq')), may hold values from -6 to 6
- cotangent: bfloat16 [16384, 768], P(('grp', 'seq')), may hold values from -6 to 6
- seq_len: int32 [8], P('grp'), may hold values from 1024 to 2048, as said below
- weight_mats: bfloat16 [768, 9280], replicated
- weight_vecs: bfloat16 [768, 13], replicated
- master_mats: float32 [768, 9280], P('grp'), may hold values from -0.21875 to 0.21875
- master_vecs: float32 [768, 13], P('grp'), may hold values from -3 to 3
- moment_mats: float32 [768, 9280], P('grp'), may hold values from -384 to 384
- moment_vecs: float32 [768, 13], P('grp'), may hold values from -384 to 384
- square_mats: float32 [768, 9280], P('grp'), may hold values from 819.2 to 32768
- square_vecs: float32 [768, 13], P('grp'), may hold values from 819.2 to 32768
- average_mats: float32 [768, 9280], P('grp'), may hold values from -0.21875 to 0.21875
- average_vecs: float32 [768, 13], P('grp'), may hold values from -3 to 3
Outputs:
- block_output: bfloat16 [16384, 768], P(('grp', 'seq'))
- input_grad: bfloat16 [16384, 768], P(('grp', 'seq'))
- grad_mats: float32 [768, 9280], P('grp')
- grad_vecs: float32 [768, 13], P('grp')
- master_mats_new: float32 [768, 9280], P('grp')
- master_vecs_new: float32 [768, 13], P('grp')
- moment_mats_new: float32 [768, 9280], P('grp')
- moment_vecs_new: float32 [768, 13], P('grp')
- square_mats_new: float32 [768, 9280], P('grp')
- square_vecs_new: float32 [768, 13], P('grp')
- average_mats_new: float32 [768, 9280], P('grp')
- average_vecs_new: float32 [768, 13], P('grp')
- copy_mats: bfloat16 [768, 9280], P('grp')
- copy_vecs: bfloat16 [768, 13], P('grp')
Inputs may be any that keep to these rules, and one draw needn't show every extreme that they name: Each group's sequences all have the length seq_len of that group; both values 2 * 512 and 2048 occur in every draw.
All inputs are finite; a program needn't handle non-finite values.
Results may differ from a plain program's by a relative error of at most 0.018.
Values may be sent and summed in bfloat16 or wider, within the bound.
No kernel may reach another device: no remote copies, remote signals or barrier semaphores. Data moves between devices by JAX's collectives and lax.ppermute only.
A program may use at most 192 MiB of HBM per device.

v0:
```python
from functools import partial
import jax
import jax.numpy as jnp
from jax import lax
from jax.sharding import PartitionSpec as P

D = 768
HEADS = 12
HD = 64
FF = 3072
norm_eps = 1e-05
adam_eps = 1e-08
beta_first = 0.5
beta_second = 0.5
learn_rate = 0.01
vector_rate = 0.06
decay_rate = 0.1
average_keep = 0.9
highest = lax.Precision.HIGHEST
careful_level = lax.Precision.HIGH


def contract_rows(left, right):
    return lax.dot_general(
        left, right, (((0,), (0,)), ((), ())), preferred_element_type=jnp.float32
    )


def contract_cols(left, right):
    return lax.dot_general(
        left, right, (((1,), (1,)), ((), ())), preferred_element_type=jnp.float32
    )


def precise(left, right):
    return jnp.dot(left, right, preferred_element_type=jnp.float32, precision=careful_level)


def norm_rows(values, gain, shift):
    average = jnp.mean(values, axis=1, keepdims=True)
    centered = values - average
    variance = jnp.mean(centered * centered, axis=1, keepdims=True)
    return centered * lax.rsqrt(variance + norm_eps) * gain + shift


def norm_back(values, gain, upstream):
    average = jnp.mean(values, axis=1, keepdims=True)
    centered = values - average
    variance = jnp.mean(centered * centered, axis=1, keepdims=True)
    inverse = lax.rsqrt(variance + norm_eps)
    normed = centered * inverse
    d_gain = jnp.sum(upstream * normed, axis=0)
    d_shift = jnp.sum(upstream, axis=0)
    d_normed = upstream * gain
    d_values = inverse * (
        d_normed
        - jnp.mean(d_normed, axis=1, keepdims=True)
        - normed * jnp.mean(d_normed * normed, axis=1, keepdims=True)
    )
    return (d_values, d_gain, d_shift)


def feature_map(values, hedge_map):
    count = values.shape[0]
    per_head = values.reshape(count, HEADS, HD)
    scores = jnp.einsum("nhi,hij->nhj", per_head, hedge_map, precision=highest)
    return jnp.concatenate(
        [jax.nn.softmax(scores, axis=-1), jax.nn.softmax(-scores, axis=-1)], axis=-1
    )


def adam_step(grad, master, first, second, rate):
    new_first = beta_first * first + (1.0 - beta_first) * grad
    new_second = beta_second * second + (1.0 - beta_second) * grad * grad
    new_master = master - rate * (
        new_first / (jnp.sqrt(new_second) + adam_eps) + decay_rate * master
    )
    return (new_master, new_first, new_second)


def on_device(
    tokens,
    cotangent,
    seq_len,
    weight_mats,
    weight_vecs,
    master_mats,
    master_vecs,
    moment_mats,
    moment_vecs,
    square_mats,
    square_vecs,
    average_mats,
    average_vecs,
):
    rows = tokens.shape[0]
    my_start = lax.axis_index("seq") * rows
    seq_length = seq_len[0]
    starts = (my_start % seq_length == 0).astype(jnp.float32)
    continued = 1.0 - starts
    w_qkv = weight_mats[:, : 3 * D]
    w_proj = weight_mats[:, 3 * D : 4 * D]
    w_fc = weight_mats[:, 4 * D : 4 * D + FF]
    w_down = weight_mats[:, 4 * D + FF : 4 * D + 2 * FF]
    hedge_map = weight_mats[:, 4 * D + 2 * FF :].astype(jnp.float32).reshape(HEADS, HD, HD)
    vec_all = weight_vecs.astype(jnp.float32)
    gain_one = vec_all[:, 0]
    gain_two = vec_all[:, 2]
    bias_qkv = vec_all[:, 6:9].T.reshape(3 * D)
    bias_fc = vec_all[:, 9:].T.reshape(FF)
    line_index = jnp.arange(rows, dtype=jnp.int32)
    causal = (line_index[:, None] >= line_index[None, :]).astype(jnp.float32)
    inputs = tokens.astype(jnp.float32)
    normed_low = norm_rows(inputs, gain_one, vec_all[:, 1]).astype(jnp.bfloat16)
    projected = jnp.dot(normed_low, w_qkv, preferred_element_type=jnp.float32) + bias_qkv
    queries = projected[:, :D]
    keys = projected[:, D : 2 * D]
    values_low = projected[:, 2 * D :].astype(jnp.bfloat16)
    query_full, query_back = jax.vjp(feature_map, queries, hedge_map)
    key_full, key_back = jax.vjp(feature_map, keys, hedge_map)
    query_feat = query_full.astype(jnp.bfloat16)
    key_feat = key_full.astype(jnp.bfloat16)
    value_heads = values_low.reshape(rows, HEADS, HD)
    gath_keys, gath_values = (
        lax.all_gather(key_feat.reshape(rows, 2 * D), "seq", axis=0, tiled=True),
        lax.all_gather(values_low, "seq", axis=0, tiled=True),
    )
    positions = jnp.arange(gath_keys.shape[0], dtype=jnp.int32)
    keep_rows = (
        (positions < my_start) & (positions // seq_length == my_start // seq_length)
    ).astype(jnp.bfloat16)
    kept_keys = (gath_keys * keep_rows[:, None]).reshape(-1, HEADS, 2 * HD)
    state_in = jnp.einsum(
        "nhf,nhd->hfd",
        kept_keys,
        gath_values.reshape(-1, HEADS, HD),
        preferred_element_type=jnp.float32,
    )
    total_in = jnp.sum(kept_keys, axis=0, dtype=jnp.float32)
    query_heads = jnp.transpose(query_feat, (1, 0, 2))
    key_heads = jnp.transpose(key_feat, (1, 0, 2))
    value_major = jnp.transpose(value_heads, (1, 0, 2))

    def attend(parts):
        query_part, key_part, value_part, state, total = parts
        query_wide = query_part.astype(jnp.float32)
        weights = jnp.dot(query_part, key_part.T, preferred_element_type=jnp.float32) * causal
        numer = precise(weights, value_part.astype(jnp.float32)) + precise(query_wide, state)
        denom = jnp.sum(weights, axis=1) + precise(query_wide, total)
        return (numer / denom[:, None], denom)

    head_outs, denoms = lax.map(attend, (query_heads, key_heads, value_major, state_in, total_in))
    mixed_low = jnp.transpose(head_outs, (1, 0, 2)).reshape(rows, D).astype(jnp.bfloat16)
    attn_out = jnp.dot(mixed_low, w_proj, preferred_element_type=jnp.float32) + vec_all[:, 4]
    resid = inputs + attn_out
    normed_two_low = norm_rows(resid, gain_two, vec_all[:, 3]).astype(jnp.bfloat16)
    hidden_pre = jnp.dot(normed_two_low, w_fc, preferred_element_type=jnp.float32) + bias_fc
    hidden_act, gelu_back = jax.vjp(partial(jax.nn.gelu, approximate=True), hidden_pre)
    hidden_low = hidden_act.astype(jnp.bfloat16)
    result = resid + contract_cols(hidden_low, w_down) + vec_all[:, 5]
    block_output = result.astype(jnp.bfloat16)
    grad_out = cotangent.astype(jnp.float32)
    d_down = contract_rows(cotangent, hidden_low)
    d_bias_down = jnp.sum(grad_out, axis=0)
    d_hidden = jnp.dot(cotangent, w_down, preferred_element_type=jnp.float32)
    d_pre_low = gelu_back(d_hidden)[0].astype(jnp.bfloat16)
    d_fc = contract_rows(normed_two_low, d_pre_low)
    d_bias_fc = jnp.sum(d_pre_low.astype(jnp.float32), axis=0)
    d_normed_two = contract_cols(d_pre_low, w_fc)
    d_resid_norm, d_gain_two, d_shift_two = norm_back(resid, gain_two, d_normed_two)
    d_resid = grad_out + d_resid_norm
    d_attn_low = d_resid.astype(jnp.bfloat16)
    d_bias_proj = jnp.sum(d_attn_low.astype(jnp.float32), axis=0)
    d_proj = contract_rows(mixed_low, d_attn_low)
    d_mixed_low = lax.optimization_barrier(contract_cols(d_attn_low, w_proj).astype(jnp.bfloat16))
    d_mixed = jnp.transpose(d_mixed_low.astype(jnp.float32).reshape(rows, HEADS, HD), (1, 0, 2))

    def attend_back(parts):
        query_part, key_part, value_part, state, total, outs, denom, upstream = parts
        query_wide = query_part.astype(jnp.float32)
        key_wide = key_part.astype(jnp.float32)
        weights = jnp.dot(query_part, key_part.T, preferred_element_type=jnp.float32) * causal
        ratio = upstream / denom[:, None]
        offset = -jnp.sum(upstream * outs, axis=1) / denom
        d_weights = (precise(ratio, value_part.astype(jnp.float32).T) + offset[:, None]) * causal
        d_query = (
            precise(d_weights, key_wide)
            + precise(ratio, state.T)
            + offset[:, None] * total[None, :]
        )
        d_key = precise(d_weights.T, query_wide)
        d_value = precise(weights.T, ratio)
        back_state = precise(query_wide.T, ratio) * continued
        back_total = precise(offset, query_wide) * continued
        return (d_query, d_key, d_value, back_state, back_total)

    d_query_h, d_key_h, d_value_h, back_state, back_total = lax.map(
        attend_back,
        (query_heads, key_heads, value_major, state_in, total_in, head_outs, denoms, d_mixed),
    )
    count = rows * lax.axis_size("seq")
    keys_part = gath_keys.astype(jnp.float32).reshape(count, HEADS, 2 * HD)
    vals_part = gath_values.astype(jnp.float32).reshape(count, HEADS, HD)
    keep_part = keep_rows.astype(jnp.float32)
    d_keys_part = (
        jnp.einsum("nhd,hfd->nhf", vals_part, back_state, precision=careful_level)
        + back_total[None]
    ) * keep_part[:, None, None]
    d_vals_part = (
        jnp.einsum("nhf,hfd->nhd", keys_part, back_state, precision=careful_level)
        * keep_part[:, None, None]
    )
    remote = lax.psum_scatter(
        jnp.concatenate(
            [d_keys_part.reshape(count, 2 * D), d_vals_part.reshape(count, D)], axis=1
        ).astype(jnp.bfloat16),
        "seq",
        scatter_dimension=0,
        tiled=True,
    ).astype(jnp.float32)
    d_key_extra = remote[:, : 2 * D].reshape(rows, HEADS, 2 * HD)
    d_value_extra = remote[:, 2 * D :].reshape(rows, HEADS, HD)
    d_query_all = jnp.transpose(d_query_h, (1, 0, 2))
    d_key_all = jnp.transpose(d_key_h, (1, 0, 2)) + d_key_extra
    d_value_all = jnp.transpose(d_value_h, (1, 0, 2)) + d_value_extra
    d_queries, d_map_query = query_back(d_query_all)
    d_keys, d_map_key = key_back(d_key_all)
    d_proj_low = jnp.concatenate([d_queries, d_keys, d_value_all.reshape(rows, D)], axis=1).astype(
        jnp.bfloat16
    )
    d_qkv = contract_rows(normed_low, d_proj_low)
    d_bias_qkv = jnp.sum(d_proj_low.astype(jnp.float32), axis=0)
    d_normed_one = contract_cols(d_proj_low, w_qkv)
    d_input_norm, d_gain_one, d_shift_one = norm_back(inputs, gain_one, d_normed_one)
    input_grad = (d_resid + d_input_norm).astype(jnp.bfloat16)
    grad_mats = jnp.concatenate(
        [d_qkv, d_proj, d_fc, d_down, (d_map_query + d_map_key).reshape(D, HD)], axis=1
    )
    grad_vecs = jnp.concatenate(
        [
            jnp.stack(
                [d_gain_one, d_shift_one, d_gain_two, d_shift_two, d_bias_proj, d_bias_down], axis=1
            ),
            d_bias_qkv.reshape(3, D).T,
            d_bias_fc.reshape(FF // D, D).T,
        ],
        axis=1,
    )
    owned_mats, owned_vecs = (
        lax.psum_scatter(grad_mats, "grp", scatter_dimension=0, tiled=True),
        lax.psum_scatter(grad_vecs, "grp", scatter_dimension=0, tiled=True),
    )
    grad_mats_own, grad_vecs_own = (
        lax.psum(owned_mats.astype(jnp.bfloat16), "seq").astype(jnp.float32),
        lax.psum(owned_vecs.astype(jnp.bfloat16), "seq").astype(jnp.float32),
    )
    new_mats, new_first_m, new_second_m = adam_step(
        grad_mats_own, master_mats, moment_mats, square_mats, learn_rate
    )
    new_vecs, new_first_v, new_second_v = adam_step(
        grad_vecs_own, master_vecs, moment_vecs, square_vecs, vector_rate
    )
    new_avg_m = average_keep * average_mats + (1.0 - average_keep) * new_mats
    new_avg_v = average_keep * average_vecs + (1.0 - average_keep) * new_vecs
    return (
        block_output,
        input_grad,
        grad_mats_own,
        grad_vecs_own,
        new_mats,
        new_vecs,
        new_first_m,
        new_first_v,
        new_second_m,
        new_second_v,
        new_avg_m,
        new_avg_v,
        new_mats.astype(jnp.bfloat16),
        new_vecs.astype(jnp.bfloat16),
    )


def solution(mesh):
    in_specs = (
        P(("grp", "seq"), None),
        P(("grp", "seq"), None),
        P("grp"),
        P(),
        P(),
        P("grp", None),
        P("grp", None),
        P("grp", None),
        P("grp", None),
        P("grp", None),
        P("grp", None),
        P("grp", None),
        P("grp", None),
    )
    out_specs = (
        P(("grp", "seq"), None),
        P(("grp", "seq"), None),
        P("grp", None),
        P("grp", None),
        P("grp", None),
        P("grp", None),
        P("grp", None),
        P("grp", None),
        P("grp", None),
        P("grp", None),
        P("grp", None),
        P("grp", None),
        P("grp", None),
        P("grp", None),
    )
    return jax.shard_map(
        on_device, mesh=mesh, in_specs=in_specs, out_specs=out_specs, check_vma=False
    )
```

profile of v0, /device:TPU:0, one launch (start us, length us, event | category | flops | bytes accessed | tf_op | source)
XLA Modules:
  0.0 1010.2 jit_solution(10283826518961896790)
XLA Ops:
  11.6 4.2 convolution_add_fusion.3
  19.1 3.3 fusion.162
  25.0 2.4 fusion.165
  45.7 3.1 copy.80
  50.2 2.6 copy.81
  53.0 12.7 %all-gather.5.cloned.1.call-done = bf16[2048,768]{1,0:T(8,128)(2,1)} async-done(((bf16[512,768]{1,0:T(8,128)(2,1)}), bf16[2048,768]{1,0:T(8,128)(2,1)}) %all-gather.5.cloned.1.call-update) | async-done | bytes 3145744 | tf_op jit(solution)/shard_map/all_gather | solution.py:126
  65.8 4.6 copy.78
  70.4 67.8 %all-gather.3.cloned.1.call-done = bf16[2048,1536]{0,1:T(8,128)(2,1)} async-done(((bf16[512,1536]{0,1:T(8,128)(2,1)}), bf16[2048,1536]{0,1:T(8,128)(2,1)}) %all-gather.3.cloned.1.call-update) | async-done | bytes 6291472 | tf_op jit(solution)/shard_map/all_gather | solution.py:125
  138.2 5.0 convert_reduce_fusion
  146.4 81.3 %while.33 = (s32[]{:T(128)}, f32[12,512,64]{1,2,0:T(8,128)}, f32[12,512]{1,0:T(8,128)}, bf16[12,512,128]{2,1,0:T(8,128)(2,1)}, bf16[12,512,128]{2,1,0:T(8,128)(2...) while((s32[]{:T(128)}, f32[12,512,64]{1,2,0:T(8,128)}, ...), condition=%wide.region_13.14_spmd.clone, body=%wide.region_11.13_spmd.clone.sunk | while | flops 194183168 | bytes 3231861 | solution.py:152
  229.5 2.4 fusion.167
  232.4 5.0 fusion.85
  237.4 11.5 %convert_reduce_fusion.1 = (f32[3072]{0:T(1024)}, bf16[512,3072]{1,0:T(8,128)(2,1)S(1)}) fusion(f32[512,3072]{1,0:T(8,128)S(1)} %fusion.85, f32[3072]{0:T(1024)S(1)} %add.216, bf16[512,768]{1,0:T(8,128)(2,1)S(1)} %copy-done.40, bf16[768,9280]{0,1:T(8,128)(2,1)} %param.20), kind=kOutput, calls=%fused_computation.105 | convolution fusion | flops 2452091904 | bytes 14966784 | tf_op jit(solution)/shard_map/dot_general | solution.py:165
  249.0 3.5 multiply_reduce_fusion
  258.5 202.7 %while.34 = (s32[]{:T(128)}, f32[12,512,128]{1,2,0:T(8,128)}, f32[12,512,128]{1,2,0:T(8,128)}, f32[12,512,64]{1,2,0:T(8,128)}, f32[12,128,64]{1,2,0:T(8,128)}, /...) while((s32[]{:T(128)}, f32[12,512,128]{1,2,0:T(8,128)}, ...), condition=%wide.region_20.21_spmd.clone.clone, body=%wide.region_18.20_spmd.clone.clone.sunk | while | flops 723526784 | bytes 10363109 | solution.py:197
  461.3 5.1 multiply_convert_fusion.1
  466.4 5.4 multiply_convert_fusion
  471.8 11.6 %pad_maximum_fusion = bf16[2048,2304]{0,1:T(8,128)(2,1)} fusion(bf16[2048,768]{0,1:T(8,128)(2,1)S(1)} %bitcast.307, bf16[2048,1536]{0,1:T(8,128)(2,1)S(1)} %bitcast.302), kind=kLoop, calls=%fused_computation.92 | loop fusion | flops 18874368 | bytes 18874368 | tf_op jit(solution)/shard_map/concatenate | solution.py:214
  484.8 3.4 multiply_reduce_fusion.4
  491.5 87.1 %reduce-scatter.6.cloned.1.call-done = bf16[512,2304]{0,1:T(8,128)(2,1)} async-done(((bf16[2048,2304]{0,1:T(8,128)(2,1)}), bf16[512,2304]{0,1:T(8,128)(2,1)}) %reduce-scatter.6.cloned.1.call-update) | async-done | bytes 2359312 | tf_op jit(solution)/shard_map/reduce_scatter | solution.py:213
  592.2 5.4 convolution_dynamic-update-slice_fusion
  600.0 5.5 convolution_dynamic-update-slice_fusion.1
  605.5 5.5 bitcast_dynamic-update-slice_fusion
  614.4 6.0 fusion.110
  621.8 270.7 %reduce-scatter.8.cloned.1.call-done = f32[96,9280]{1,0:T(8,128)} async-done(((f32[768,9280]{1,0:T(8,128)}), f32[96,9280]{1,0:T(8,128)}) %reduce-scatter.8.cloned.1.call-update) | async-done | bytes 3563536 | tf_op jit(solution)/shard_map/reduce_scatter | solution.py:250
  892.5 3.4 convert_element_type.146
  896.6 9.6 add_convert_fusion
  907.7 16.4 %reduce-scatter.10.cloned.1.call-done = f32[96,13]{1,0:T(8,128)} async-done(((f32[768,13]{1,0:T(8,128)}), f32[96,13]{1,0:T(8,128)}) %reduce-scatter.10.cloned.1.call-update) | async-done | bytes 5008
  925.0 10.0 psum.15
  936.3 54.8 %all-reduce.2.cloned.1.call-done = bf16[96,9280]{1,0:T(8,128)(2,1)} async-done(((bf16[96,9280]{1,0:T(8,128)(2,1)}), bf16[96,9280]{1,0:T(8,128)(2,1)}) %all-reduce.2.cloned.1.call-update) | async-done | bytes 1781776 | tf_op jit(solution)/shard_map/psum | solution.py:254
  991.1 8.9 fusion.158
  1000.1 2.8 multiply_add_fusion.1
  (577 shorter events, 353.1 us)
Async XLA Ops:
  7.2 58.6 %all-gather.5.cloned.1.call-start = ((), (), s32[]{:S(2)}) async-start(), calls=%async_computation.4 | async-start | bytes 3932160 | tf_op jit(solution)/shard_map/all_gather | solution.py:126
  8.7 7.1 copy-start.53
  8.7 7.1 copy-start.71
  8.7 223.7 %copy-start.69 = (f32[768]{0:T(1024)}, f32[768]{0:T(1024)S(1)}, u32[]{:S(2)}) copy-start(f32[768]{0:T(1024)S(1)} %get-tuple-element.327) | copy-start | bytes 9220
  8.7 243.8 %copy-start.51 = (f32[768]{0:T(1024)}, f32[768]{0:T(1024)S(1)}, u32[]{:S(2)}) copy-start(f32[768]{0:T(1024)S(1)} %get-tuple-element.325) | copy-start | bytes 9220
  10.0 5.7 copy-start.45
  18.9 119.3 %all-gather.3.cloned.1.call-start = ((), (), s32[]{:S(2)}) async-start(), calls=%async_computation.3 | async-start | bytes 7864320 | tf_op jit(solution)/shard_map/all_gather | solution.py:125
  19.1 18.3 %copy-start.30 = (bf16[768,64]{1,0:T(8,128)(2,1)}, bf16[768,64]{1,0:T(8,128)(2,1)S(1)}, u32[]{:S(2)}) copy-start(bf16[768,64]{1,0:T(8,128)(2,1)S(1)} %copy.136) | copy-start | bytes 294916
  32.5 546.0 %reduce-scatter.6.cloned.1.call-start = ((), (), s32[]{:S(2)}) async-start(), calls=%async_computation.5 | async-start | bytes 11796480 | tf_op jit(solution)/shard_map/reduce_scatter | solution.py:213
  34.0 203.4 %copy-start.55 = (f32[3072]{0:T(1024)}, f32[3072]{0:T(1024)S(1)}, u32[]{:S(2)}) copy-start(f32[3072]{0:T(1024)S(1)} %add.216) | copy-start | bytes 36868
  232.0 20.5 %copy-start.27 = (f32[512,768]{1,0:T(8,128)}, f32[512,768]{1,0:T(8,128)S(1)}, u32[]{:S(2)}) copy-start(f32[512,768]{1,0:T(8,128)S(1)} %get-tuple-element.409) | copy-start | bytes 4718596
  232.0 20.5 %copy-start.47 = (f32[512]{0:T(512)}, f32[512]{0:T(512)S(1)}, u32[]{:S(2)}) copy-start(f32[512]{0:T(512)S(1)} %broadcast_multiply_fusion.5) | copy-start | bytes 6148
  232.3 20.2 %copy-start.60 = (f32[512]{0:T(512)}, f32[512]{0:T(512)S(1)}, u32[]{:S(2)}) copy-start(f32[512]{0:T(512)S(1)} %add_rsqrt_fusion) | copy-start | bytes 6148
  232.4 16.6 %slice-start = ((s8[14254080]{0:T(1024)(128)(4,1)}), s8[4194304]{0:T(1024)(128)(4,1)S(1)}, s32[]{:S(2)}) async-start(s8[14254080]{0:T(1024)(128)(4,1)} %bitcast.338), calls=%async_computation.9 | async-start | bytes 8388608
  232.4 16.6 %slice-start.1 = ((s8[14254080]{0:T(1024)(128)(4,1)}), s8[4194304]{0:T(1024)(128)(4,1)S(1)}, s32[]{:S(2)}) async-start(s8[14254080]{0:T(1024)(128)(4,1)} %bitcast.338), calls=%async_computation.10 | async-start | bytes 8388608
  237.4 11.5 %copy-start.78 = (f32[512,3072]{1,0:T(8,128)}, f32[512,3072]{1,0:T(8,128)S(1)}, u32[]{:S(2)}) copy-start(f32[512,3072]{1,0:T(8,128)S(1)} %fusion.85) | copy-start | bytes 18874372
  237.4 11.5 %slice-start.2 = ((s8[14254080]{0:T(1024)(128)(4,1)}), s8[4194304]{0:T(1024)(128)(4,1)S(1)}, s32[]{:S(2)}) async-start(s8[14254080]{0:T(1024)(128)(4,1)} %bitcast.338), calls=%async_computation.11 | async-start | bytes 8388608
  237.4 11.5 %slice-start.3 = ((s8[14254080]{0:T(1024)(128)(4,1)}), s8[1671168]{0:T(1024)(128)(4,1)S(1)}, s32[]{:S(2)}) async-start(s8[14254080]{0:T(1024)(128)(4,1)} %bitcast.338), calls=%async_computation.12 | async-start | bytes 3342336
  483.4 409.1 %reduce-scatter.8.cloned.1.call-start = ((), (), s32[]{:S(2)}) async-start(), calls=%async_computation.6 | async-start | bytes 32292864 | tf_op jit(solution)/shard_map/reduce_scatter | solution.py:250
  591.5 6.2 copy-start.38
  592.2 7.7 copy-start.77
  597.7 7.8 slice-start.5
  599.9 5.6 copy-start.41
  611.9 312.3 %reduce-scatter.10.cloned.1.call-start = ((), (), s32[]{:S(2)}) async-start(), calls=%async_computation.8 | async-start | bytes 442368
  621.5 369.6 %all-reduce.2.cloned.1.call-start = ((), (), s32[]{:S(2)}) async-start(), calls=%async_computation.7 | async-start | bytes 3588096 | tf_op jit(solution)/shard_map/psum | solution.py:254
  896.6 9.6 copy-start.39
  906.2 28.8 %copy-start.63 = (f32[96,13]{0,1:T(8,128)S(1)}, f32[96,13]{0,1:T(8,128)}, u32[]{:S(2)}) copy-start(f32[96,13]{0,1:T(8,128)} %param.23) | copy-start | bytes 14980
  906.2 28.8 %copy-start.64 = (f32[96,13]{0,1:T(8,128)S(1)}, f32[96,13]{0,1:T(8,128)}, u32[]{:S(2)}) copy-start(f32[96,13]{0,1:T(8,128)} %param.27) | copy-start | bytes 14980
  906.3 28.8 %copy-start.65 = (f32[96,13]{0,1:T(8,128)S(1)}, f32[96,13]{0,1:T(8,128)}, u32[]{:S(2)}) copy-start(f32[96,13]{0,1:T(8,128)} %param.25) | copy-start | bytes 14980
  906.3 29.4 %copy-start.62 = (f32[96,13]{0,1:T(8,128)S(1)}, f32[96,13]{0,1:T(8,128)}, u32[]{:S(2)}) copy-start(f32[96,13]{0,1:T(8,128)} %param.29) | copy-start | bytes 14980
  935.7 64.4 %copy-start.44 = (f32[96,13]{0,1:T(8,128)}, f32[96,13]{0,1:T(8,128)S(1)}, u32[]{:S(2)}) copy-start(f32[96,13]{0,1:T(8,128)S(1)} %get-tuple-element.378) | copy-start | bytes 14980
  991.1 8.9 copy-start.32
  (71 other events, 170.4 us)
Sparse Core Ops, SparseCore 0:
  19.0 46.6 all-gather.4
  68.2 70.0 all-gather.2
  483.5 95.0 reduce-scatter.5
  612.0 280.4 reduce-scatter.7
  895.2 28.9 reduce-scatter.9
  928.2 62.9 all-reduce.1
where the time goes:
time: 1020 us; the launch traced here: 1010 us
  waiting for transfers between devices  510 us (50%)
  matrix products  282 us (28%)
  local copies, waits for them, and re-layouts  123 us (12%)
  other arithmetic  67.8 us (7%)
  between operations  16.2 us (2%)
    reduce_scatter x1, waiting for transfers between devices, on_device(): lax.psum_scatter(grad_mats, 'grp', scatter_dimension=0, tiled=True)  271 us
    dot_general x120, matrix products, precise(): jnp.dot(left, right, preferred_element_type=jnp.float32, precision=carefu...  171 us
    reduce_scatter x1, waiting for transfers between devices, on_device(): lax.psum_scatter(jnp.concatenate([d_keys_part.reshape(count, 2 * D), d_va...  87.1 us
    all_gather x1, waiting for transfers between devices, on_device(): lax.all_gather(key_feat.reshape(rows, 2 * D), 'seq', axis=0, tiled=True)  67.8 us
    psum x1, waiting for transfers between devices, on_device(): lax.psum(owned_mats.astype(jnp.bfloat16), 'seq').astype(jnp.float32)  54.8 us
    dynamic_update_slice x36, local copies, waits for them, and re-layouts, on_device(): lax.map(attend_back, (query_heads, key_heads, value_major, state_in, tota...  25.7 us
    dynamic_slice x48, local copies, waits for them, and re-layouts, on_device(): lax.map(attend_back, (query_heads, key_heads, value_major, state_in, tota...  23.5 us
    unnamed x173, local copies, waits for them, and re-layouts  23.3 us
  transfers between devices with their start and end apart: 6, of which 6 were waited for; matrix products, arithmetic and copies ran while one was open for 7% of the time, Pallas kernels for 0%

commit v1 on v0

--- a/solution.py
+++ b/solution.py
@@ -18,6 +18,11 @@
 average_keep = 0.9
 highest = lax.Precision.HIGHEST
 careful_level = lax.Precision.HIGH
+
+
+def gather_over(x, name, along):
+    stack = jnp.stack([x] * lax.axis_size(name))
+    return jnp.concatenate(lax.all_to_all(stack, name, 0, 0), axis=along)
 
 
 def contract_rows(left, right):
@@ -122,7 +127,7 @@
     key_feat = key_full.astype(jnp.bfloat16)
     value_heads = values_low.reshape(rows, HEADS, HD)
     gath_keys, gath_values = (
-        lax.all_gather(key_feat.reshape(rows, 2 * D), "seq", axis=0, tiled=True),
+        gather_over(key_feat.reshape(rows, 2 * D), "seq", 0),
         lax.all_gather(values_low, "seq", axis=0, tiled=True),
     )
     positions = jnp.arange(gath_keys.shape[0], dtype=jnp.int32)

time: 1020 us -> 1050 us (1.029)
  local copies, waits for them, and re-layouts: 123 us -> 147 us
    all_to_all x0 -> x1, waiting for transfers between devices: none -> 73.1 us  [gather_over(): return jnp.concatenate(lax.all_to_all(stack, name, 0, 0), axis=along)]
    all_gather x1 -> x0, waiting for transfers between devices: 67.8 us -> none  [on_device(): lax.all_gather(key_feat.reshape(rows, 2 * D), 'seq', axis=0, tiled=True)]
    all_gather x1, waiting for transfers between devices: 12.7 us -> 0.01 us  [on_device(): lax.all_gather(values_low, 'seq', axis=0, tiled=True)]
    reshape x0 -> x1, local copies, waits for them, and re-layouts: none -> 11 us  [gather_over(): return jnp.concatenate(lax.all_to_all(stack, name, 0, 0), axis=along)]
    all_to_all x0 -> x1, local copies, waits for them, and re-layouts: none -> 10.5 us  [gather_over(): return jnp.concatenate(lax.all_to_all(stack, name, 0, 0), axis=along)]
    unnamed x173 -> x169, local copies, waits for them, and re-layouts: 23.3 us -> 22.7 us
  transfers between devices with their start and end apart: 6 -> 6, of which waited for: 6 -> 5; matrix products, arithmetic and copies ran while one was open for 7% -> 7% of each run, Pallas kernels for 0% -> 0%
where the time goes in v1:
time: 1050 us; the launch traced here: 1030 us
  waiting for transfers between devices  503 us (48%)
  matrix products  286 us (27%)
  local copies, waits for them, and re-layouts  147 us (14%)
  other arithmetic  66.1 us (6%)
  between operations  15.9 us (2%)
    reduce_scatter x1, waiting for transfers between devices, on_device(): lax.psum_scatter(grad_mats, 'grp', scatter_dimension=0, tiled=True)  271 us
    dot_general x120, matrix products, precise(): jnp.dot(left, right, preferred_element_type=jnp.float32, precision=carefu...  170 us
    reduce_scatter x1, waiting for transfers between devices, on_device(): lax.psum_scatter(jnp.concatenate([d_keys_part.reshape(count, 2 * D), d_va...  87.5 us
    all_to_all x1, waiting for transfers between devices, gather_over(): return jnp.concatenate(lax.all_to_all(stack, name, 0, 0), axis=along)  73.1 us
    psum x1, waiting for transfers between devices, on_device(): lax.psum(owned_mats.astype(jnp.bfloat16), 'seq').astype(jnp.float32)  54.8 us
    dynamic_update_slice x36, local copies, waits for them, and re-layouts, on_device(): lax.map(attend_back, (query_heads, key_heads, value_major, state_in, tota...  25.7 us
    dynamic_slice x48, local copies, waits for them, and re-layouts, on_device(): lax.map(attend_back, (query_heads, key_heads, value_major, state_in, tota...  23.5 us
    unnamed x169, local copies, waits for them, and re-layouts  22.7 us
  transfers between devices with their start and end apart: 6, of which 5 were waited for; matrix products, arithmetic and copies ran while one was open for 7% of the time, Pallas kernels for 0%

profile of v1, /device:TPU:0, one launch (start us, length us, event | category | flops | bytes accessed | tf_op | source)
XLA Modules:
  0.0 1034.5 jit_solution(14767387564600683333)
XLA Ops:
  11.7 4.2 convolution_add_fusion.3
  28.2 3.2 stack.21
  31.4 5.2 all-to-all-start
  53.2 2.7 copy.82
  60.2 73.1 %all-to-all-done = bf16[4,512,1536]{1,2,0:T(8,128)(2,1)} async-done(((bf16[4,512,1536]{1,2,0:T(8,128)(2,1)}), bf16[4,512,1536]{1,2,0:T(8,128)(2,1)}, u32[]{:S(2)}, u32[]{:S(2)}) %all-to-all-start) | async-done | bytes 6291488 | tf_op jit(solution)/shard_map/all_to_all | solution.py:25
  133.3 10.5 %copy.79 = bf16[4,512,1536]{1,0,2:T(4,128)(2,1)} copy(bf16[4,512,1536]{1,2,0:T(8,128)(2,1)} %all-to-all-done) | data formatting | bytes 12582912 | tf_op jit(solution)/shard_map/all_to_all | solution.py:25
  143.8 11.0 %reshape.287 = bf16[2048,12,128]{0,2,1:T(8,128)(2,1)} reshape(bf16[4,512,1536]{1,0,2:T(4,128)(2,1)} %copy.79) | data formatting | bytes 12582912 | tf_op jit(solution)/shard_map/reshape | solution.py:25
  154.9 4.6 copy.80
  159.5 5.5 fusion.79
  165.0 4.7 convert_reduce_fusion
  171.0 81.3 %while.33 = (s32[]{:T(128)}, f32[12,512,64]{1,2,0:T(8,128)}, f32[12,512]{1,0:T(8,128)}, bf16[12,512,128]{2,1,0:T(8,128)(2,1)}, bf16[12,512,128]{2,1,0:T(8,128)(2...) while((s32[]{:T(128)}, f32[12,512,64]{1,2,0:T(8,128)}, ...), condition=%wide.region_13.14_spmd.clone, body=%wide.region_11.13_spmd.clone.sunk | while | flops 194183168 | bytes 3231861 | solution.py:157
  257.0 5.0 fusion.87
  262.1 11.5 %convert_reduce_fusion.1 = (f32[3072]{0:T(1024)}, bf16[512,3072]{1,0:T(8,128)(2,1)S(1)}) fusion(f32[512,3072]{1,0:T(8,128)S(1)} %fusion.87, f32[3072]{0:T(1024)S(1)} %add.221, bf16[512,768]{1,0:T(8,128)(2,1)S(1)} %copy-done.38, bf16[768,9280]{0,1:T(8,128)(2,1)} %param.20), kind=kOutput, calls=%fused_computation.105 | convolution fusion | flops 2452091904 | bytes 14966784 | tf_op jit(solution)/shard_map/dot_general | solution.py:170
  273.6 3.5 multiply_reduce_fusion
  283.2 202.2 %while.34 = (s32[]{:T(128)}, f32[12,512,128]{1,2,0:T(8,128)}, f32[12,512,128]{1,2,0:T(8,128)}, f32[12,512,64]{1,2,0:T(8,128)}, f32[12,128,64]{1,2,0:T(8,128)}, /...) while((s32[]{:T(128)}, f32[12,512,128]{1,2,0:T(8,128)}, ...), condition=%wide.region_20.21_spmd.clone.clone, body=%wide.region_18.20_spmd.clone.clone.sunk | while | flops 723526784 | bytes 10363109 | solution.py:202
  485.5 5.1 multiply_convert_fusion.1
  490.6 5.4 multiply_convert_fusion
  496.0 11.6 %pad_maximum_fusion = bf16[2048,2304]{0,1:T(8,128)(2,1)} fusion(bf16[2048,768]{0,1:T(8,128)(2,1)S(1)} %bitcast.305, bf16[2048,1536]{0,1:T(8,128)(2,1)S(1)} %bitcast.300), kind=kLoop, calls=%fused_computation.92 | loop fusion | flops 18874368 | bytes 18874368 | tf_op jit(solution)/shard_map/concatenate | solution.py:219
  509.0 3.4 multiply_reduce_fusion.4
  515.7 87.5 %reduce-scatter.6.cloned.1.call-done = bf16[512,2304]{0,1:T(8,128)(2,1)} async-done(((bf16[2048,2304]{0,1:T(8,128)(2,1)}), bf16[512,2304]{0,1:T(8,128)(2,1)}) %reduce-scatter.6.cloned.1.call-update) | async-done | bytes 2359312 | tf_op jit(solution)/shard_map/reduce_scatter | solution.py:218
  616.8 5.4 convolution_dynamic-update-slice_fusion
  624.6 5.5 convolution_dynamic-update-slice_fusion.1
  630.2 5.5 bitcast_dynamic-update-slice_fusion
  639.1 6.0 fusion.113
  646.5 270.7 %reduce-scatter.8.cloned.1.call-done = f32[96,9280]{1,0:T(8,128)} async-done(((f32[768,9280]{1,0:T(8,128)}), f32[96,9280]{1,0:T(8,128)}) %reduce-scatter.8.cloned.1.call-update) | async-done | bytes 3563536 | tf_op jit(solution)/shard_map/reduce_scatter | solution.py:255
  917.2 3.4 convert_element_type.151
  921.3 9.6 add_convert_fusion
  932.4 16.5 %reduce-scatter.10.cloned.1.call-done = f32[96,13]{1,0:T(8,128)} async-done(((f32[768,13]{1,0:T(8,128)}), f32[96,13]{1,0:T(8,128)}) %reduce-scatter.10.cloned.1.call-update) | async-done | bytes 5008
  949.8 9.9 psum.15
  961.0 54.8 %all-reduce.2.cloned.1.call-done = bf16[96,9280]{1,0:T(8,128)(2,1)} async-done(((bf16[96,9280]{1,0:T(8,128)(2,1)}), bf16[96,9280]{1,0:T(8,128)(2,1)}) %all-reduce.2.cloned.1.call-update) | async-done | bytes 1781776 | tf_op jit(solution)/shard_map/psum | solution.py:259
  1015.8 8.9 fusion.166
  1024.8 2.7 multiply_add_fusion.1
  (575 shorter events, 360.9 us)
Async XLA Ops:
  8.7 7.3 copy-start.51
  8.7 7.3 copy-start.69
  8.7 248.3 %copy-start.67 = (f32[768]{0:T(1024)}, f32[768]{0:T(1024)S(1)}, u32[]{:S(2)}) copy-start(f32[768]{0:T(1024)S(1)} %get-tuple-element.327) | copy-start | bytes 9220
  8.7 268.4 %copy-start.49 = (f32[768]{0:T(1024)}, f32[768]{0:T(1024)S(1)}, u32[]{:S(2)}) copy-start(f32[768]{0:T(1024)S(1)} %get-tuple-element.325) | copy-start | bytes 9220
  10.0 6.0 copy-start.43
  11.7 33.2 %copy-start.28 = (bf16[768,64]{1,0:T(8,128)(2,1)}, bf16[768,64]{1,0:T(8,128)(2,1)S(1)}, u32[]{:S(2)}) copy-start(bf16[768,64]{1,0:T(8,128)(2,1)S(1)} %copy.138) | copy-start | bytes 294916
  31.4 102.0 %all-to-all-start = ((bf16[4,512,1536]{1,2,0:T(8,128)(2,1)}), bf16[4,512,1536]{1,2,0:T(8,128)(2,1)}, u32[]{:S(2)}, u32[]{:S(2)}) async-start(bf16[4,512,1536]{1,2,0:T(8,128)(2,1)} %stack.21), calls=%async_computation | async-start | bytes 12582912 | tf_op jit(solution)/shard_map/all_to_all | solution.py:25
  36.6 118.3 %all-gather.2.cloned.1.call-start = ((), (), s32[]{:S(2)}) async-start(), calls=%async_computation.4 | async-start | bytes 3932160 | tf_op jit(solution)/shard_map/all_gather | solution.py:131
  39.0 564.1 %reduce-scatter.6.cloned.1.call-start = ((), (), s32[]{:S(2)}) async-start(), calls=%async_computation.5 | async-start | bytes 11796480 | tf_op jit(solution)/shard_map/reduce_scatter | solution.py:218
  41.5 220.5 %copy-start.53 = (f32[3072]{0:T(1024)}, f32[3072]{0:T(1024)S(1)}, u32[]{:S(2)}) copy-start(f32[3072]{0:T(1024)S(1)} %add.221) | copy-start | bytes 36868
  256.6 20.5 %copy-start.25 = (f32[512,768]{1,0:T(8,128)}, f32[512,768]{1,0:T(8,128)S(1)}, u32[]{:S(2)}) copy-start(f32[512,768]{1,0:T(8,128)S(1)} %get-tuple-element.407) | copy-start | bytes 4718596
  256.6 20.5 %copy-start.45 = (f32[512]{0:T(512)}, f32[512]{0:T(512)S(1)}, u32[]{:S(2)}) copy-start(f32[512]{0:T(512)S(1)} %broadcast_multiply_fusion.4) | copy-start | bytes 6148
  256.9 20.2 %copy-start.58 = (f32[512]{0:T(512)}, f32[512]{0:T(512)S(1)}, u32[]{:S(2)}) copy-start(f32[512]{0:T(512)S(1)} %add_rsqrt_fusion) | copy-start | bytes 6148
  257.0 16.6 %slice-start = ((s8[14254080]{0:T(1024)(128)(4,1)}), s8[4194304]{0:T(1024)(128)(4,1)S(1)}, s32[]{:S(2)}) async-start(s8[14254080]{0:T(1024)(128)(4,1)} %bitcast.336), calls=%async_computation.9 | async-start | bytes 8388608
  257.0 16.6 %slice-start.1 = ((s8[14254080]{0:T(1024)(128)(4,1)}), s8[4194304]{0:T(1024)(128)(4,1)S(1)}, s32[]{:S(2)}) async-start(s8[14254080]{0:T(1024)(128)(4,1)} %bitcast.336), calls=%async_computation.10 | async-start | bytes 8388608
  262.0 11.5 %copy-start.76 = (f32[512,3072]{1,0:T(8,128)}, f32[512,3072]{1,0:T(8,128)S(1)}, u32[]{:S(2)}) copy-start(f32[512,3072]{1,0:T(8,128)S(1)} %fusion.87) | copy-start | bytes 18874372
  262.0 11.5 %slice-start.2 = ((s8[14254080]{0:T(1024)(128)(4,1)}), s8[4194304]{0:T(1024)(128)(4,1)S(1)}, s32[]{:S(2)}) async-start(s8[14254080]{0:T(1024)(128)(4,1)} %bitcast.336), calls=%async_computation.11 | async-start | bytes 8388608
  262.0 11.5 %slice-start.3 = ((s8[14254080]{0:T(1024)(128)(4,1)}), s8[1671168]{0:T(1024)(128)(4,1)S(1)}, s32[]{:S(2)}) async-start(s8[14254080]{0:T(1024)(128)(4,1)} %bitcast.336), calls=%async_computation.12 | async-start | bytes 3342336
  507.6 409.6 %reduce-scatter.8.cloned.1.call-start = ((), (), s32[]{:S(2)}) async-start(), calls=%async_computation.6 | async-start | bytes 32292864 | tf_op jit(solution)/shard_map/reduce_scatter | solution.py:255
  616.1 6.2 copy-start.36
  616.8 7.8 copy-start.75
  622.3 7.9 slice-start.5
  624.6 5.6 copy-start.39
  636.6 312.4 %reduce-scatter.10.cloned.1.call-start = ((), (), s32[]{:S(2)}) async-start(), calls=%async_computation.8 | async-start | bytes 442368
  646.2 369.6 %all-reduce.2.cloned.1.call-start = ((), (), s32[]{:S(2)}) async-start(), calls=%async_computation.7 | async-start | bytes 3588096 | tf_op jit(solution)/shard_map/psum | solution.py:259
  921.3 9.6 copy-start.37
  930.9 28.8 %copy-start.61 = (f32[96,13]{0,1:T(8,128)S(1)}, f32[96,13]{0,1:T(8,128)}, u32[]{:S(2)}) copy-start(f32[96,13]{0,1:T(8,128)} %param.23) | copy-start | bytes 14980
  930.9 28.8 %copy-start.62 = (f32[96,13]{0,1:T(8,128)S(1)}, f32[96,13]{0,1:T(8,128)}, u32[]{:S(2)}) copy-start(f32[96,13]{0,1:T(8,128)} %param.27) | copy-start | bytes 14980
  930.9 28.8 %copy-start.63 = (f32[96,13]{0,1:T(8,128)S(1)}, f32[96,13]{0,1:T(8,128)}, u32[]{:S(2)}) copy-start(f32[96,13]{0,1:T(8,128)} %param.25) | copy-start | bytes 14980
  930.9 29.4 %copy-start.60 = (f32[96,13]{0,1:T(8,128)S(1)}, f32[96,13]{0,1:T(8,128)}, u32[]{:S(2)}) copy-start(f32[96,13]{0,1:T(8,128)} %param.29) | copy-start | bytes 14980
  960.4 64.4 %copy-start.42 = (f32[96,13]{0,1:T(8,128)}, f32[96,13]{0,1:T(8,128)S(1)}, u32[]{:S(2)}) copy-start(f32[96,13]{0,1:T(8,128)S(1)} %get-tuple-element.378) | copy-start | bytes 14980
  1015.8 8.9 copy-start.30
  (69 other events, 166.9 us)
Sparse Core Ops, SparseCore 0:
  39.8 93.1 all-gather.1
  507.7 95.4 reduce-scatter.5
  636.7 280.4 reduce-scatter.7
  919.8 29.0 reduce-scatter.9
  952.9 62.8 all-reduce.1
